TPU v7x, 256 devices: a whole 4x4x8 slice. The times are simulated.
256 devices in a mesh: group: 8 (over x, z_lo), replica: 32 (over y, z_hi, core).
Axes of the slice: x: 4, y: 4, z: 8 (z_hi: 4, z_lo: 2; z = z_hi * 2 + z_lo), core: 2. Of those that a mesh axis runs over, the one named last changes fastest.
Arguments:
- hidden_in: bfloat16 [81920, 3072], P(('group', 'replica')), may hold values from -24 to 24
- w_query: bfloat16 [3072, 1536], replicated, may hold values from -0.109375 to 0.109375
- query_gain: float32 [128], replicated, may hold values from 0.5 to 2
- down_projection_matrix: bfloat16 [3072, 64], replicated, may hold values from -0.23925781 to 0.23925781
- up_projection_matrix: bfloat16 [64, 1536], replicated, may hold values from -0.59765625 to 0.59765625
- query_cotangent: bfloat16 [81920, 1536], P(('group', 'replica')), may hold values from -24 to 24
- first_moment: float32 [4608, 64], P(('group', 'replica')), may hold values from -3 to 3
- second_moment: float32 [4608, 64], P(('group', 'replica')), may hold values from 0.001 to 0.1
Outputs:
- new_down: bfloat16 [3072, 64], replicated
- new_up: bfloat16 [64, 1536], replicated
- first_next: float32 [4608, 64], P(('group', 'replica'))
- second_next: float32 [4608, 64], P(('group', 'replica'))
All inputs are finite; a program needn't handle non-finite values.
Results may differ from a plain program's by a relative error of at most 0.0019.
Values may be sent and summed in bfloat16 or wider, within the bound.
A program may use at most 64 MiB of HBM per device.

v0:
```python
import jax
import jax.numpy as jnp
from jax import lax
from jax.sharding import PartitionSpec as P

adapter_scale_factor = 0.5
norm_epsilon = 1e-06
beta_one = 0.9
beta_two = 0.999
first_bias = 1.0 - 0.9**10
second_bias = 1.0 - 0.999**10
learn_rate = 0.001
adam_eps = 1e-08


def queries_backward(
    rows_in, grads_in, w_query, query_gain, down_projection_matrix, up_projection_matrix
):
    reduced_rank_input = jnp.dot(
        rows_in, down_projection_matrix, preferred_element_type=jnp.float32
    ).astype(jnp.bfloat16)
    apply_projection = jnp.dot(rows_in, w_query, preferred_element_type=jnp.float32)
    apply_projection = apply_projection + adapter_scale_factor * jnp.dot(
        reduced_rank_input, up_projection_matrix, preferred_element_type=jnp.float32
    )
    token_count = apply_projection.shape[0]
    head_size = query_gain.shape[0]
    shaped = apply_projection.reshape(token_count, -1, head_size)
    inverse = lax.rsqrt(jnp.mean(shaped * shaped, axis=-1, keepdims=True) + norm_epsilon)
    normed = shaped * inverse
    upstream = grads_in.astype(jnp.float32).reshape(shaped.shape) * query_gain
    grad_pre = inverse * (upstream - normed * jnp.mean(upstream * normed, axis=-1, keepdims=True))
    grad_pre = grad_pre.reshape(token_count, -1).astype(jnp.bfloat16)
    backward_reduced = lax.dot_general(
        grad_pre, up_projection_matrix, (((1,), (1,)), ((), ())), preferred_element_type=jnp.float32
    )
    backward_reduced = (adapter_scale_factor * backward_reduced).astype(jnp.bfloat16)
    scaled_reduced = (reduced_rank_input.astype(jnp.float32) * adapter_scale_factor).astype(
        jnp.bfloat16
    )
    return (grad_pre, backward_reduced, scaled_reduced)


def adam_update(grads, params, first, second):
    first_new = beta_one * first + (1.0 - beta_one) * grads
    second_new = beta_two * second + (1.0 - beta_two) * grads * grads
    direction = first_new / first_bias / (jnp.sqrt(second_new / second_bias) + adam_eps)
    return ((params - learn_rate * direction).astype(jnp.bfloat16), first_new, second_new)


def on_device(
    hidden_in,
    w_query,
    query_gain,
    down_projection_matrix,
    up_projection_matrix,
    query_cotangent,
    first_moment,
    second_moment,
):
    model_width = hidden_in.shape[1]
    adapter_rank_size = down_projection_matrix.shape[1]
    row_count_total = model_width + up_projection_matrix.shape[1]
    accelerator_list = lax.axis_size("group") * lax.axis_size("replica")
    own_rows = row_count_total // accelerator_list
    grad_pre, backward_reduced, scaled_reduced = queries_backward(
        hidden_in,
        query_cotangent,
        w_query,
        query_gain,
        down_projection_matrix,
        up_projection_matrix,
    )
    stacked = jnp.concatenate([hidden_in, grad_pre], axis=1)
    operand = jnp.concatenate([backward_reduced, scaled_reduced], axis=1)
    matrix_product = lax.dot_general(
        stacked, operand, (((0,), (0,)), ((), ())), preferred_element_type=jnp.float32
    )
    row_ids = lax.iota(jnp.int32, lax.axis_size(("group", "replica")) * own_rows)
    is_down_matrix = (row_ids < model_width)[:, None]
    grad_own = lax.psum_scatter(
        jnp.where(
            is_down_matrix,
            matrix_product[:, :adapter_rank_size],
            matrix_product[:, adapter_rank_size:],
        )
        / accelerator_list,
        ("group", "replica"),
        scatter_dimension=0,
        tiled=True,
    )
    owner = lax.axis_index(("group", "replica"))
    combined = jnp.concatenate([down_projection_matrix, up_projection_matrix.T], axis=0)
    params_own = lax.dynamic_slice_in_dim(combined, owner * own_rows, own_rows, 0).astype(
        jnp.float32
    )
    updated_own, first_new, second_new = adam_update(
        grad_own, params_own, first_moment, second_moment
    )
    gathered = lax.all_gather(updated_own, ("group", "replica"), axis=0, tiled=True)
    return (gathered[:model_width], gathered[model_width:].T, first_new, second_new)


def solution(mesh):
    placed = (
        P(("group", "replica"), None),
        P(),
        P(),
        P(),
        P(),
        P(("group", "replica"), None),
        P(("group", "replica"), None),
        P(("group", "replica"), None),
    )
    return jax.shard_map(
        on_device,
        mesh=mesh,
        in_specs=placed,
        out_specs=(P(), P(), P(("group", "replica"), None), P(("group", "replica"), None)),
        check_vma=False,
    )
```

profile of v0, /device:TPU:1, one launch (start us, length us, event | category | flops | bytes accessed | tf_op | source)
XLA Modules:
  0.0 660.7 jit_solution(2586570845125717426)
XLA Ops:
  7.2 0.0 all-reduce.3.cloned.1.call-start
  7.2 3.1 multiply_convert_fusion.1
  10.3 5.8 fusion.15
  16.1 1.7 fusion.4
  17.8 2.0 copy.42
  19.8 0.2 multiply_reduce_fusion.1
  20.0 0.6 add_rsqrt_fusion
  20.6 0.4 copy-done.3
  21.0 1.7 copy.44
  22.7 0.7 broadcast_bitcast_fusion
  23.4 2.2 multiply_reduce_fusion
  25.6 0.2 mul.117
  25.7 1.9 copy.45
  27.6 2.3 mul.106
  29.9 3.1 copy.46
  33.1 3.0 multiply_convert_fusion
  36.1 0.4 fusion.6
  36.5 0.8 fusion
  37.3 0.0 copy-start.5
  37.3 1.2 fusion.5
  38.5 0.0 all-reduce.3.cloned.1.call-update
  38.5 0.4 copy.41
  38.9 0.2 copy.40
  39.2 261.5 %all-reduce.3.cloned.1.call-done = f32[4608,64]{0,1:T(8,128)} async-done(((f32[4608,64]{0,1:T(8,128)}), f32[4608,64]{0,1:T(8,128)}) %all-reduce.3.cloned.1.call-update) | async-done | bytes 1179664
  300.7 0.9 constant_dynamic-slice_fusion
  301.6 0.1 copy.47
  301.7 0.6 fusion.12
  302.3 349.1 %all-gather = bf16[256,18,64]{2,1,0:T(8,128)(2,1)S(1)} all-gather(bf16[1,18,64]{2,1,0:T(8,128)(2,1)S(1)} %get-tuple-element.20), channel_id=1, replica_groups=mesh['group'=8,'replica'=32] {'group','replica'}, dimensions={0}, use_global_device_ids=true | all-gather | bytes 592128 | tf_op jit(solution)/shard_map/all_gather | solution.py:100
  651.4 0.6 reshape.39
  651.9 0.1 slice.18
  652.0 1.0 copy.50
  653.0 0.8 copy.51
  (19 shorter events, 0.1 us)
Async XLA Ops:
  7.2 3.1 copy-start.1
  7.2 293.5 %all-reduce.3.cloned.1.call-start = ((), (), s32[]{:S(2)}) async-start(), calls=%async_computation | async-start | bytes 2359296
  10.3 5.8 copy-start.4
  19.8 1.2 copy-start.3
  29.9 3.1 copy-start
  33.0 3.5 copy-start.2
  33.1 3.5 copy-start.6
  37.3 1.2 copy-start.5
  38.5 263.2 %copy-start.7 = (f32[18,64]{1,0:T(8,128)S(1)}, f32[18,64]{1,0:T(8,128)}, u32[]{:S(2)}) copy-start(f32[18,64]{1,0:T(8,128)} %param.14) | copy-start | bytes 13828
  38.5 263.2 %copy-start.8 = (f32[18,64]{1,0:T(8,128)S(1)}, f32[18,64]{1,0:T(8,128)}, u32[]{:S(2)}) copy-start(f32[18,64]{1,0:T(8,128)} %param.15) | copy-start | bytes 13828
Sparse Core Ops, SparseCore 0:
  38.6 261.9 all-reduce.2
where the time goes:
time: 661 us
  blocking collectives  349 us (53%)
  waiting for transfers between devices  262 us (40%)
  local copies, waits for them, and re-layouts  16.3 us (2%)
  between operations  14.2 us (2%)
  matrix products  11.7 us (2%)
  other arithmetic  7.86 us (1%)
    all_gather x1, blocking collectives, on_device(): lax.all_gather(updated_own, ('group', 'replica'), axis=0, tiled=True)  349 us
    unnamed x2, waiting for transfers between devices  262 us
  transfers between devices with their start and end apart: 1, of which 1 were waited for; matrix products, arithmetic and copies ran while one was open for 0% of the time, Pallas kernels for 0%

commit v1 on v0

--- a/solution.py
+++ b/solution.py
@@ -97,7 +97,15 @@
     updated_own, first_new, second_new = adam_update(
         grad_own, params_own, first_moment, second_moment
     )
-    gathered = lax.all_gather(updated_own, ("group", "replica"), axis=0, tiled=True)
+    gathered = jnp.concatenate(
+        lax.all_to_all(
+            jnp.stack([updated_own] * lax.axis_size(("group", "replica"))),
+            ("group", "replica"),
+            0,
+            0,
+        ),
+        axis=0,
+    )
     return (gathered[:model_width], gathered[model_width:].T, first_new, second_new)
 
 

time: 661 us -> 349 us (0.53)
  blocking collectives: 349 us -> 34.9 us
    all_gather x1 -> x0, blocking collectives: 349 us -> none  [on_device(): lax.all_gather(updated_own, ('group', 'replica'), axis=0, tiled=True)]
    all_to_all x0 -> x1, blocking collectives: none -> 34.9 us  [on_device(): lax.all_to_all(jnp.stack([updated_own] * lax.axis_size(('group', 'replica...]
where the time goes in v1:
time: 349 us
  waiting for transfers between devices  262 us (75%)
  blocking collectives  34.9 us (10%)
  local copies, waits for them, and re-layouts  18.4 us (5%)
  between operations  14.3 us (4%)
  matrix products  11.7 us (3%)
  other arithmetic  7.86 us (2%)
    unnamed x2, waiting for transfers between devices  262 us
    all_to_all x1, blocking collectives, on_device(): lax.all_to_all(jnp.stack([updated_own] * lax.axis_size(('group', 'replica...  34.9 us
  transfers between devices with their start and end apart: 1, of which 1 were waited for; matrix products, arithmetic and copies ran while one was open for 0% of the time, Pallas kernels for 0%

profile of v1, /device:TPU:1, one launch (start us, length us, event | category | flops | bytes accessed | tf_op | source)
XLA Modules:
  0.0 348.7 jit_solution(13554343984495735929)
XLA Ops:
  7.2 3.1 multiply_convert_fusion.1
  10.3 5.8 %fusion.14 = f32[320,1536]{1,0:T(8,128)S(1)} fusion(bf16[320,3072]{1,0:T(8,128)(2,1)S(1)} %copy-done.1, bf16[3072,1536]{1,0:T(8,128)(2,1)} %param.9), kind=kOutput, calls=%fused_computation.32 | convolution fusion | flops 3019898880 | bytes 13369344 | tf_op jit(solution)/shard_map/dot_general | solution.py:22
  16.1 1.7 fusion.4
  17.8 2.0 copy.42
  19.8 0.2 multiply_reduce_fusion.1
  20.0 0.6 add_rsqrt_fusion
  20.6 0.4 copy-done.3
  21.0 1.7 copy.44
  22.7 0.7 broadcast_bitcast_fusion
  23.4 2.2 multiply_reduce_fusion
  25.6 0.2 mul.117
  25.7 1.9 copy.45
  27.6 2.3 mul.106
  29.9 3.1 copy.46
  33.1 3.0 multiply_convert_fusion
  36.1 0.4 fusion.6
  36.5 0.8 fusion
  37.3 1.2 fusion.5
  38.5 0.4 copy.41
  38.9 0.2 copy.40
  39.2 261.5 %all-reduce.3.cloned.1.call-done = f32[4608,64]{0,1:T(8,128)} async-done(((f32[4608,64]{0,1:T(8,128)}), f32[4608,64]{0,1:T(8,128)}) %all-reduce.3.cloned.1.call-update) | async-done | bytes 1179664
  300.7 0.9 constant_dynamic-slice_fusion
  301.6 0.1 copy.47
  301.7 0.6 subtract_convert_fusion
  302.3 0.2 stack.2
  302.5 0.9 reshape.46
  303.4 34.9 %all_to_all.5 = bf16[256,2,576]{2,1,0:T(2,128)(2,1)S(1)} all-to-all(bf16[256,2,576]{2,1,0:T(2,128)(2,1)S(1)} %reshape.46), channel_id=1, replica_groups=mesh['group'=8,'replica'=32] {'group','replica'}, dimensions={0} | all-to-all | bytes 1179648 | tf_op jit(solution)/shard_map/all_to_all | solution.py:101
  338.3 1.0 reshape.47
  339.3 0.6 reshape.43
  339.9 0.1 slice.18
  340.0 1.0 copy.50
  341.0 0.8 copy.51
  (22 shorter events, 0.1 us)
Async XLA Ops:
  7.2 3.1 copy-start.1
  7.2 293.5 %all-reduce.3.cloned.1.call-start = ((), (), s32[]{:S(2)}) async-start(), calls=%async_computation.1 | async-start | bytes 2359296
  10.3 5.8 %copy-start.4 = (bf16[64,1536]{1,0:T(8,128)(2,1)S(1)}, bf16[64,1536]{1,0:T(8,128)(2,1)}, u32[]{:S(2)}) copy-start(bf16[64,1536]{1,0:T(8,128)(2,1)} %param.12) | copy-start | bytes 589828
  19.8 1.2 copy-start.3
  29.9 3.1 copy-start
  33.0 3.5 copy-start.2
  33.1 3.5 copy-start.6
  37.3 1.2 copy-start.5
  38.5 263.2 %copy-start.7 = (f32[18,64]{1,0:T(8,128)S(1)}, f32[18,64]{1,0:T(8,128)}, u32[]{:S(2)}) copy-start(f32[18,64]{1,0:T(8,128)} %param.14) | copy-start | bytes 13828
  38.5 263.2 %copy-start.8 = (f32[18,64]{1,0:T(8,128)S(1)}, f32[18,64]{1,0:T(8,128)}, u32[]{:S(2)}) copy-start(f32[18,64]{1,0:T(8,128)} %param.15) | copy-start | bytes 13828
Sparse Core Ops, SparseCore 0:
  38.6 261.9 all-reduce.2
